TPU v7x, 256 devices: a whole 4x4x8 slice. The times are simulated.
256 devices in a mesh: blk: 16 (over z, x_hi), leaf: 8 (over y, core), rhs: 2 (over x_lo).
Axes of the slice: x: 4 (x_hi: 2, x_lo: 2; x = x_hi * 2 + x_lo), y: 4, z: 8, core: 2. Of those that a mesh axis runs over, the one named last changes fastest.
Arguments:
- residual: float32 [32, 8, 65536], P('rhs', 'leaf', 'blk'), may hold values from -160 to 160
- points: float32 [3, 8, 65536], P(None, 'leaf', 'blk'), may hold values from -12330 to 12330
- noise: float32 [8, 65536], P('leaf', 'blk'), may hold values from 1 to 2
- block_list: int32 [8, 8, 256], P('leaf'), may hold values from 0 to 1, as said below
Outputs:
- correction: float32 [32, 8, 65536], P('rhs', 'leaf', 'blk')
- new_residual: float32 [32, 8, 65536], P('rhs', 'leaf', 'blk')
- basis: float32 [128, 8, 65536], P('rhs', 'leaf', 'blk')
Inputs may be any that keep to these rules, and one draw needn't show every extreme that they name: The list is symmetric: block_list[t, k, i] == block_list[t, 7 - k, (i + d) mod 256] with d the offset of entry k.
All inputs are finite; a program needn't handle non-finite values.
Results may differ from a plain program's by a relative error of at most 0.007.
Values sent between devices are 32-bit elements; how exact they have to be, the bound alone decides.
A program may use at most 128 MiB of HBM per device.

v0:
```python
import jax
import jax.numpy as jnp
from jax import lax
from jax.sharding import PartitionSpec as P

M = 32
S = 4
BS = 256
REACH = 4
SUPPORT = 1408
centre_shift = 1.5
amplitude = 1.1
exact = lax.Precision.HIGHEST


def extended(x, sides, width):
    for axis, dim in sides:
        count, length = (lax.axis_size(axis), x.shape[dim])
        up = [(i, (i + 1) % count) for i in range(count)]
        down = [(j, i) for i, j in up]
        last = lax.slice_in_dim(x, length - width, length, axis=dim)
        leading = lax.slice_in_dim(x, 0, width, axis=dim)
        before = lax.ppermute(last, axis, up)
        after = lax.ppermute(leading, axis, down)
        x = jnp.concatenate([before, x, after], axis=dim)
    return x


def kernel_tile(near_points, own_points):
    squared = (near_points[0][:, None] - own_points[0][None, :]) ** 2
    squared = squared + (near_points[1][:, None] - own_points[1][None, :]) ** 2
    squared = squared + (near_points[2][:, None] - own_points[2][None, :]) ** 2
    radius = jnp.sqrt(squared) / SUPPORT
    remain = jnp.maximum(1.0 - radius, 0.0)
    return remain * remain * (remain * remain) * (4.0 * radius + 1.0) * (amplitude / SUPPORT)


def band_product(field_wide, points_wide, weights, rows_out):
    per_turn = rows_out // 8
    count = field_wide.shape[0]

    def turn(carry, index):
        pieces = []
        for inner in range(per_turn):
            block = index * per_turn + inner
            own_points = lax.dynamic_slice_in_dim(points_wide, (block + REACH) * BS, BS, 1)
            total = jnp.zeros((count, BS), jnp.float32)
            for offset in range(2 * REACH + 1):
                column_at = (block + offset) * BS
                near_points = lax.dynamic_slice_in_dim(points_wide, column_at, BS, 1)
                near_field = lax.dynamic_slice_in_dim(field_wide, column_at, BS, 1)
                listed = lax.dynamic_index_in_dim(weights[offset], block, 0, False)
                tile = kernel_tile(near_points, own_points) * listed
                total = total + jnp.dot(near_field, tile, precision=exact)
            pieces.append(total)
        return (carry, jnp.concatenate(pieces, axis=1))

    carry, parts = lax.scan(turn, jnp.zeros((), jnp.int32), jnp.arange(8, dtype=jnp.int32))
    return jnp.moveaxis(parts, 0, 1).reshape(count, rows_out * BS)


def galerkin(gram, count_points, count_sides):
    normed = gram / count_points
    basis_count = normed.shape[0] - count_sides
    gram_basis = normed[:basis_count, :basis_count]
    factor_low = jnp.linalg.cholesky(gram_basis)
    inverse_low = lax.linalg.triangular_solve(
        factor_low, jnp.eye(basis_count, dtype=jnp.float32), left_side=True, lower=True
    )
    cross = normed[:basis_count, count_sides:] + centre_shift * gram_basis
    projected = jnp.dot(
        jnp.dot(inverse_low, cross, precision=exact), inverse_low.T, precision=exact
    )
    projected = 0.5 * (projected + projected.T)
    small_side = jnp.dot(inverse_low, gram_basis[:, :count_sides], precision=exact)
    proj_factor = jnp.linalg.cholesky(projected)
    halfway = lax.linalg.triangular_solve(proj_factor, small_side, left_side=True, lower=True)
    coeffs = lax.linalg.triangular_solve(
        proj_factor, halfway, left_side=True, lower=True, transpose_a=True
    )
    combo = jnp.dot(coeffs.T, inverse_low, precision=exact)
    return (inverse_low, combo)


def row_products(rows):
    return lax.dot_general(rows, rows, (((1,), (1,)), ((), ())), precision=exact)


def local(residual, points, noise, block_list):
    field = residual[:, 0]
    coords = points[:, 0]
    nugget = noise[0]
    own_rows = field.shape[1]
    own_blocks = own_rows // BS
    first_block = lax.axis_index("blk") * own_blocks
    listed = block_list[0].astype(jnp.float32)
    nine = jnp.concatenate(
        [listed[:REACH], jnp.ones((1, listed.shape[1]), jnp.float32), listed[REACH:]], axis=0
    )
    margin = S * REACH
    wrapped = jnp.concatenate([nine[:, -margin:], nine, nine[:, :margin]], axis=1)
    powers = [field]
    rim = REACH * BS
    coords_wide = extended(coords, (("blk", 1),), rim)
    own_weights = lax.dynamic_slice_in_dim(wrapped, first_block + margin, own_blocks, 1)
    current = field
    for power_step in range(S):
        widened = extended(current, (("blk", 1),), rim)
        current = (
            band_product(widened, coords_wide, own_weights, own_blocks)
            + (nugget - centre_shift) * current
        )
        powers.append(current)
    half_panel = jnp.stack(powers, axis=0)
    count_points = own_rows * lax.axis_size("blk") * lax.axis_size("leaf")
    sides_here = field.shape[0]
    whole = lax.all_gather(half_panel, "rhs", axis=1, tiled=True)
    flat = whole.reshape(-1, own_rows)
    gram = lax.psum(row_products(flat), ("blk", "leaf"))
    inverse_low, combo = galerkin(gram, count_points, M)
    first_rows = flat[: S * M]
    image = flat[M:] + centre_shift * first_rows
    part = lax.axis_index("rhs")
    basis_here = S * M // lax.axis_size("rhs")
    mine_low = lax.dynamic_slice_in_dim(inverse_low, part * basis_here, basis_here, 0)
    mine_combo = lax.dynamic_slice_in_dim(combo, part * sides_here, sides_here, 0)
    correction = jnp.dot(mine_combo, first_rows, precision=exact)
    new_residual = field - jnp.dot(mine_combo, image, precision=exact)
    basis = jnp.dot(mine_low, first_rows, precision=exact)
    return (correction[:, None], new_residual[:, None], basis[:, None])


def solution(mesh):
    placed = (
        P("rhs", "leaf", "blk"),
        P(None, "leaf", "blk"),
        P("leaf", "blk"),
        P("leaf", None, None),
    )
    return jax.shard_map(
        local,
        mesh=mesh,
        in_specs=placed,
        out_specs=(P("rhs", "leaf", "blk"), P("rhs", "leaf", "blk"), P("rhs", "leaf", "blk")),
        check_vma=False,
    )
```

profile of v0, /device:TPU:2, one launch (start us, length us, event | category | flops | bytes accessed | tf_op | source)
XLA Modules:
  0.0 2114.2 jit_solution(17787421845742051918)
XLA Ops:
  8.1 2.2 collective-permute-start.2
  10.3 5.4 collective-permute-start.3
  15.6 1.1 copy.47
  16.9 5.6 collective-permute-start.1
  22.5 1.1 bitcast_dynamic-update-slice_fusion
  25.4 206.0 %while.52 = (s32[]{:T(128)}, f32[8,16,512]{2,1,0:T(8,128)S(1)}, s32[8]{0:T(128)S(1)}, f32[16,6144]{1,0:T(8,128)S(1)}, f32[3,6144]{1,0:T(4,128)S(1)}, /*index=5*/...) while((s32[]{:T(128)}, f32[8,16,512]{2,1,0:T(8,128)S(1)}, ...), condition=%wide.region_1.2_spmd, body=%wide.region_0.1_spmd.sunk | while | flops 246620224 | bytes 1092197 | solution.py:58
  231.9 5.6 collective-permute-start.5
  237.9 1.8 collective-permute-done.4
  239.8 202.8 %while.53 = (s32[]{:T(128)}, f32[8,16,512]{2,1,0:T(8,128)S(1)}, s32[8]{0:T(128)S(1)}, f32[16,6144]{1,0:T(8,128)S(1)}, f32[3,6144]{1,0:T(4,128)S(1)}, /*index=5*/...) while((s32[]{:T(128)}, f32[8,16,512]{2,1,0:T(8,128)S(1)}, ...), condition=%wide.region_3.4_spmd, body=%wide.region_2.3_spmd.sunk | while | flops 246620224 | bytes 1092197 | solution.py:58
  442.8 6.1 collective-permute-start.7
  449.2 1.5 collective-permute-done.6
  450.9 203.8 %while.54 = (s32[]{:T(128)}, f32[8,16,512]{2,1,0:T(8,128)S(1)}, s32[8]{0:T(128)S(1)}, f32[16,6144]{1,0:T(8,128)S(1)}, f32[3,6144]{1,0:T(4,128)S(1)}, /*index=5*/...) while((s32[]{:T(128)}, f32[8,16,512]{2,1,0:T(8,128)S(1)}, ...), condition=%wide.region_5.6_spmd, body=%wide.region_4.5_spmd.sunk | while | flops 246620224 | bytes 1092197 | solution.py:58
  654.8 1.9 collective-permute-start.8
  656.7 4.4 collective-permute-start.9
  661.4 1.8 collective-permute-done.8
  663.4 207.7 %while.55 = (s32[]{:T(128)}, f32[8,16,512]{2,1,0:T(8,128)S(1)}, s32[8]{0:T(128)S(1)}, f32[16,6144]{1,0:T(8,128)S(1)}, f32[3,6144]{1,0:T(4,128)S(1)}, /*index=5*/...) while((s32[]{:T(128)}, f32[8,16,512]{2,1,0:T(8,128)S(1)}, ...), condition=%wide.region_7.8_spmd, body=%wide.region_6.7_spmd.sunk | while | flops 246620224 | bytes 1092197 | solution.py:58
  871.3 1.0 copy-done.4
  872.7 45.1 %all-gather.2.cloned.1.call-done = f32[5,32,4096]{2,1,0:T(8,128)} async-done(((f32[5,16,4096]{2,1,0:T(8,128)}), f32[5,32,4096]{2,1,0:T(8,128)}) %all-gather.2.cloned.1.call-update) | async-done | bytes 2621456 | tf_op jit(solution)/shard_map/all_gather | solution.py:117
  917.8 5.6 fusion.2577
  923.9 1.3 copy-done.1
  925.2 1.6 bitcast_add_fusion
  926.8 1122.0 %all-reduce.2.cloned.1.call-done = f32[160,160]{0,1:T(8,128)} async-done(((f32[160,160]{0,1:T(8,128)}), f32[160,160]{0,1:T(8,128)}) %all-reduce.2.cloned.1.call-update) | async-done | bytes 102416 | tf_op jit(solution)/shard_map/psum | solution.py:119
  2049.9 11.7 cholesky.44
  2062.9 9.8 custom-call.10
  2074.0 12.0 cholesky.55
  2087.3 9.8 custom-call.11
  2097.8 2.7 fusion.2532
  2100.6 1.0 copy.29
  2101.6 1.1 convolution_bitcast_fusion.1
  2102.7 1.2 convolution_bitcast_fusion
  2103.9 2.0 copy.30
  2105.9 1.0 copy.28
  (952 shorter events, 424.7 us)
Async XLA Ops:
  7.2 910.6 %all-gather.2.cloned.1.call-start = ((), (), s32[]{:S(2)}) async-start(), calls=%async_computation | async-start | bytes 3932160 | tf_op jit(solution)/shard_map/all_gather | solution.py:117
  8.1 17.2 collective-permute-start.2
  10.3 15.0 collective-permute-start.3
  16.8 8.5 collective-permute-start
  16.9 8.4 collective-permute-start.1
  25.4 206.0 %copy-start.3 = (f32[16,1,4096]{2,1,0:T(1,128)S(1)}, f32[16,1,4096]{2,1,0:T(1,128)}, u32[]{:S(2)}) copy-start(f32[16,1,4096]{2,1,0:T(1,128)} %param.13) | copy-start | bytes 786436
  231.6 8.2 collective-permute-start.4
  231.9 7.9 collective-permute-start.5
  442.7 8.0 collective-permute-start.6
  442.8 8.0 collective-permute-start.7
  654.8 8.4 collective-permute-start.8
  656.7 6.6 collective-permute-start.9
  871.3 1.1 copy-start.4
  872.4 1176.4 %all-reduce.2.cloned.1.call-start = ((), (), s32[]{:S(2)}) async-start(), calls=%async_computation.1 | async-start | bytes 327680 | tf_op jit(solution)/shard_map/psum | solution.py:119
  917.8 5.6 copy-start
  923.9 1.3 copy-start.1
  2073.9 27.7 %copy-start.2 = (f32[4,32,4096]{2,1,0:T(8,128)S(1)}, f32[4,32,4096]{2,1,0:T(8,128)}, u32[]{:S(2)}) copy-start(f32[4,32,4096]{2,1,0:T(8,128)} %copy-done.1) | copy-start | bytes 6291460
Sparse Core Ops, SparseCore 0:
  872.5 45.1 all-gather.1
  923.5 1125.2 all-reduce.1
where the time goes:
time: 2130 us; the launch traced here: 2110 us
  waiting for transfers between devices  1170 us (55%)
  loops' own time  407 us (19%)
  matrix products  296 us (14%)
  local copies, waits for them, and re-layouts  140 us (7%)
  other arithmetic  51.7 us (2%)
  starting transfers between devices  32 us (2%)
    psum x1, waiting for transfers between devices, local(): gram = lax.psum(row_products(flat), ('blk', 'leaf'))  1120 us
    another operation x4, loops' own time, band_product(): lax.scan(turn, jnp.zeros((), jnp.int32), jnp.arange(8, dtype=jnp.int32))  407 us
    dot_general x576, matrix products, turn(): total = total + jnp.dot(near_field, tile, precision=exact)  284 us
    dynamic_slice x160, local copies, waits for them, and re-layouts, turn(): listed = lax.dynamic_index_in_dim(weights[offset], block, 0, False)  105 us
    all_gather x1, waiting for transfers between devices, local(): whole = lax.all_gather(half_panel, 'rhs', axis=1, tiled=True)  45.1 us
  transfers between devices with their start and end apart: 12, of which 7 were waited for; matrix products, arithmetic and copies ran while one was open for 0% of the time, Pallas kernels for 0%

commit v1 on v0

--- a/solution.py
+++ b/solution.py
@@ -116,7 +116,9 @@
     sides_here = field.shape[0]
     whole = lax.all_gather(half_panel, "rhs", axis=1, tiled=True)
     flat = whole.reshape(-1, own_rows)
-    gram = lax.psum(row_products(flat), ("blk", "leaf"))
+    value = row_products(flat)
+    terms = lax.all_gather(value, ("blk", "leaf"), axis=0, tiled=False)
+    gram = terms.sum(axis=0)
     inverse_low, combo = galerkin(gram, count_points, M)
     first_rows = flat[: S * M]
     image = flat[M:] + centre_shift * first_rows

time: 2130 us -> 1190 us (0.56)
  waiting for transfers between devices: 1170 us -> 215 us
  loops' own time: 407 us -> 429 us
    psum x1 -> x0, waiting for transfers between devices: 1120 us -> none  [local(): gram = lax.psum(row_products(flat), ('blk', 'leaf'))]
    all_gather x0 -> x1, waiting for transfers between devices: none -> 164 us  [local(): terms = lax.all_gather(value, ('blk', 'leaf'), axis=0, tiled=False)]
    another operation x4, loops' own time: 407 us -> 429 us  [band_product(): lax.scan(turn, jnp.zeros((), jnp.int32), jnp.arange(8, dtype=jnp.int32))]
  transfers between devices with their start and end apart: 12 -> 12, of which waited for: 7 -> 7; matrix products, arithmetic and copies ran while one was open for 0% -> 1% of each run, Pallas kernels for 0% -> 0%
where the time goes in v1:
time: 1190 us; the launch traced here: 1180 us
  loops' own time  429 us (36%)
  matrix products  282 us (24%)
  waiting for transfers between devices  215 us (18%)
  local copies, waits for them, and re-layouts  143 us (12%)
  other arithmetic  59.3 us (5%)
  starting transfers between devices  31.8 us (3%)
  between operations  15 us (1%)
    another operation x4, loops' own time, band_product(): lax.scan(turn, jnp.zeros((), jnp.int32), jnp.arange(8, dtype=jnp.int32))  429 us
    dot_general x576, matrix products, turn(): total = total + jnp.dot(near_field, tile, precision=exact)  272 us
    all_gather x1, waiting for transfers between devices, local(): terms = lax.all_gather(value, ('blk', 'leaf'), axis=0, tiled=False)  164 us
    dynamic_slice x160, local copies, waits for them, and re-layouts, turn(): listed = lax.dynamic_index_in_dim(weights[offset], block, 0, False)  107 us
    all_gather x1, waiting for transfers between devices, local(): whole = lax.all_gather(half_panel, 'rhs', axis=1, tiled=True)  45.3 us
    ppermute x5, starting transfers between devices, extended(): after = lax.ppermute(leading, axis, down)  27.2 us
  transfers between devices with their start and end apart: 12, of which 7 were waited for; matrix products, arithmetic and copies ran while one was open for 1% of the time, Pallas kernels for 0%

profile of v1, /device:TPU:2, one launch (start us, length us, event | category | flops | bytes accessed | tf_op | source)
XLA Modules:
  0.0 1175.2 jit_solution(12501122035800270083)
XLA Ops:
  8.1 2.2 collective-permute-start.2
  10.3 5.4 collective-permute-start.3
  15.6 1.1 copy.58
  16.9 5.6 collective-permute-start.1
  22.5 1.1 bitcast_dynamic-update-slice_fusion
  25.4 208.2 %while.52 = (s32[]{:T(128)}, f32[8,16,512]{2,1,0:T(8,128)S(1)}, s32[8]{0:T(128)S(1)}, f32[16,6144]{1,0:T(8,128)S(1)}, f32[3,6144]{1,0:T(4,128)S(1)}, /*index=5*/...) while((s32[]{:T(128)}, f32[8,16,512]{2,1,0:T(8,128)S(1)}, ...), condition=%wide.region_1.2_spmd, body=%wide.region_0.1_spmd.sunk | while | flops 246620224 | bytes 1092189 | solution.py:58
  234.1 5.6 collective-permute-start.5
  240.1 1.8 collective-permute-done.4
  242.1 208.9 %while.53 = (s32[]{:T(128)}, f32[8,16,512]{2,1,0:T(8,128)S(1)}, s32[8]{0:T(128)S(1)}, f32[16,6144]{1,0:T(8,128)S(1)}, f32[3,6144]{1,0:T(4,128)S(1)}, /*index=5*/...) while((s32[]{:T(128)}, f32[8,16,512]{2,1,0:T(8,128)S(1)}, ...), condition=%wide.region_3.4_spmd, body=%wide.region_2.3_spmd.sunk | while | flops 246620224 | bytes 1092189 | solution.py:58
  451.2 6.1 collective-permute-start.7
  457.5 1.5 collective-permute-done.6
  459.3 207.4 %while.54 = (s32[]{:T(128)}, f32[8,16,512]{2,1,0:T(8,128)S(1)}, s32[8]{0:T(128)S(1)}, f32[16,6144]{1,0:T(8,128)S(1)}, f32[3,6144]{1,0:T(4,128)S(1)}, /*index=5*/...) while((s32[]{:T(128)}, f32[8,16,512]{2,1,0:T(8,128)S(1)}, ...), condition=%wide.region_5.6_spmd, body=%wide.region_4.5_spmd.sunk | while | flops 246620224 | bytes 1092189 | solution.py:58
  666.8 1.9 collective-permute-start.8
  668.7 4.4 collective-permute-start.9
  673.4 1.8 collective-permute-done.8
  675.4 208.7 %while.55 = (s32[]{:T(128)}, f32[8,16,512]{2,1,0:T(8,128)S(1)}, s32[8]{0:T(128)S(1)}, f32[16,6144]{1,0:T(8,128)S(1)}, f32[3,6144]{1,0:T(4,128)S(1)}, /*index=5*/...) while((s32[]{:T(128)}, f32[8,16,512]{2,1,0:T(8,128)S(1)}, ...), condition=%wide.region_7.8_spmd, body=%wide.region_6.7_spmd.sunk | while | flops 246620224 | bytes 1092189 | solution.py:58
  884.4 1.1 copy-done.5
  885.5 45.3 %all-gather.4.cloned.1.call-done = f32[5,32,4096]{2,1,0:T(8,128)} async-done(((f32[5,16,4096]{2,1,0:T(8,128)}), f32[5,32,4096]{2,1,0:T(8,128)}) %all-gather.4.cloned.1.call-update) | async-done | bytes 2621456 | tf_op jit(solution)/shard_map/all_gather | solution.py:117
  930.8 5.6 fusion.2577
  937.0 1.4 copy-done.1
  938.3 1.6 bitcast_add_fusion
  939.9 164.0 %all-gather.6.cloned.1.call-done = f32[20480,160]{1,0:T(8,128)} async-done(((f32[160,160]{1,0:T(8,128)}), f32[20480,160]{1,0:T(8,128)}) %all-gather.6.cloned.1.call-update) | async-done | bytes 13107216 | tf_op jit(solution)/shard_map/all_gather | solution.py:120
  1103.9 8.5 reduce_sum.9
  1112.6 11.7 cholesky.44
  1125.7 9.8 custom-call.10
  1136.3 1.2 convolution_bitcast_fusion
  1137.5 2.0 copy.42
  1140.1 11.9 %cholesky.55 = f32[128,128]{1,0:T(8,128)S(1)} custom-call(f32[128,128]{1,0:T(8,128)S(1)} %fusion.2542), custom_call_target="Cholesky" | custom-call | tf_op jit(solution)/shard_map/jit(cholesky)/cholesky | solution.py:76
  1153.3 9.8 custom-call.11
  1163.7 1.1 convolution_bitcast_fusion.1
  1164.9 1.1 fusion.2532
  1166.0 1.0 copy.41
  (956 shorter events, 415.4 us)
Async XLA Ops:
  7.2 923.7 %all-gather.4.cloned.1.call-start = ((), (), s32[]{:S(2)}) async-start(), calls=%async_computation | async-start | bytes 3932160 | tf_op jit(solution)/shard_map/all_gather | solution.py:117
  8.1 17.2 %collective-permute-start.2 = (f32[3,1024]{1,0:T(4,128)S(1)}, f32[3,1024]{1,0:T(4,128)S(1)}, u32[]{:S(2)}, u32[]{:S(2)}) collective-permute-start(f32[3,1024]{1,0:T(4,128)S(1)} %get-tuple-element.901), channel_id=1, source_target_pairs={{0,16},{16,32},{32,48},{48,64},{64,80},{80,96},{96,112},{112,128},... | collective-permute-start | bytes 36872 | tf_op jit(solution)/shard_map/ppermute | solution.py:23
  10.3 15.0 %collective-permute-start.3 = (f32[3,1024]{1,0:T(4,128)S(1)}, f32[3,1024]{1,0:T(4,128)S(1)}, u32[]{:S(2)}, u32[]{:S(2)}) collective-permute-start(f32[3,1024]{1,0:T(4,128)S(1)} %get-tuple-element.902), channel_id=1, source_target_pairs={{16,0},{32,16},{48,32},{64,48},{80,64},{96,80},{112,96},{128,112},... | collective-permute-start | bytes 36872 | tf_op jit(solution)/shard_map/ppermute | solution.py:24
  16.8 8.5 collective-permute-start
  16.9 8.4 collective-permute-start.1
  25.4 208.2 %copy-start.4 = (f32[16,1,4096]{2,1,0:T(1,128)S(1)}, f32[16,1,4096]{2,1,0:T(1,128)}, u32[]{:S(2)}) copy-start(f32[16,1,4096]{2,1,0:T(1,128)} %param.13) | copy-start | bytes 786436
  233.8 8.2 collective-permute-start.4
  234.1 7.9 collective-permute-start.5
  451.1 8.0 collective-permute-start.6
  451.2 8.0 collective-permute-start.7
  666.8 8.4 collective-permute-start.8
  668.7 6.6 collective-permute-start.9
  884.3 1.1 copy-start.5
  885.5 218.4 %all-gather.6.cloned.1.call-start = ((), (), s32[]{:S(2)}) async-start(), calls=%async_computation.1 | async-start | bytes 21135360 | tf_op jit(solution)/shard_map/all_gather | solution.py:120
  930.8 5.6 copy-start
  937.0 1.4 copy-start.1
  1103.9 32.4 %copy-start.2 = (f32[4,32,4096]{2,1,0:T(8,128)S(1)}, f32[4,32,4096]{2,1,0:T(8,128)}, u32[]{:S(2)}) copy-start(f32[4,32,4096]{2,1,0:T(8,128)} %copy-done.1) | copy-start | bytes 6291460
  1163.2 1.7 copy-start.3
Sparse Core Ops, SparseCore 0:
  885.6 45.1 all-gather.3
  936.6 167.2 all-gather.5
